TPU v7x, 32 devices: a whole 2x2x4 slice. The times are simulated.
32 devices in a mesh: dp: 4 (over y, x), tensor: 8 (over z, core).
Axes of the slice: x: 2, y: 2, z: 4, core: 2. Of those that a mesh axis runs over, the one named last changes fastest.
Arguments:
- tokens: bfloat16 [2, 6144, 2048], P(None, ('dp', 'tensor')), may hold values from -6 to 6
- cotangent: bfloat16 [2, 6144, 2048], P(None, ('dp', 'tensor')), may hold values from -6 to 6
- lengths: int32 [2, 4, 6], P(None, 'dp'), may hold values from 1 to 1024, 1536 in all within a row
- places: int32 [2, 4, 1536], P(None, 'dp'), may hold values from 0 to 1535, each once within a row
- owners: int32 [4, 4], replicated, may hold values from 0 to 3, each once within a row
- qkv_weight: float32 [3, 2048, 2048], P(None, 'dp', 'tensor'), may hold values from -0.1875 to 0.1875
- qkv_first: float32 [3, 2048, 2048], P(None, 'dp', 'tensor'), may hold values from -1280 to 1280
- qkv_second: float32 [3, 2048, 2048], P(None, 'dp', 'tensor'), may hold values from 49152 to 196608
- out_weight: float32 [2048, 2048], P('tensor', 'dp'), may hold values from -0.375 to 0.375
- out_first: float32 [2048, 2048], P('tensor', 'dp'), may hold values from -320 to 320
- out_second: float32 [2048, 2048], P('tensor', 'dp'), may hold values from 3072 to 12288
- proj_weight: float32 [2, 2048, 8192], P(None, 'dp', 'tensor'), may hold values from -0.125 to 0.125
- proj_first: float32 [2, 2048, 8192], P(None, 'dp', 'tensor'), may hold values from -192 to 192
- proj_second: float32 [2, 2048, 8192], P(None, 'dp', 'tensor'), may hold values from 1105.92 to 4423.68
- down_weight: float32 [8192, 2048], P('tensor', 'dp'), may hold values from -0.0625 to 0.0625
- down_first: float32 [8192, 2048], P('tensor', 'dp'), may hold values from -384 to 384
- down_second: float32 [8192, 2048], P('tensor', 'dp'), may hold values from 4423.68 to 17694.72
Outputs:
- output: bfloat16 [2, 6144, 2048], P(None, ('dp', 'tensor'))
- input_grad: float32 [2, 6144, 2048], P(None, ('dp', 'tensor'))
- qkv_grad: float32 [3, 2048, 2048], P(None, 'dp', 'tensor')
- qkv_first_next: float32 [3, 2048, 2048], P(None, 'dp', 'tensor')
- qkv_second_next: float32 [3, 2048, 2048], P(None, 'dp', 'tensor')
- qkv_master: float32 [3, 2048, 2048], P(None, 'dp', 'tensor')
- out_grad: float32 [2048, 2048], P('tensor', 'dp')
- out_first_next: float32 [2048, 2048], P('tensor', 'dp')
- out_second_next: float32 [2048, 2048], P('tensor', 'dp')
- out_master: float32 [2048, 2048], P('tensor', 'dp')
- proj_grad: float32 [2, 2048, 8192], P(None, 'dp', 'tensor')
- proj_first_next: float32 [2, 2048, 8192], P(None, 'dp', 'tensor')
- proj_second_next: float32 [2, 2048, 8192], P(None, 'dp', 'tensor')
- proj_master: float32 [2, 2048, 8192], P(None, 'dp', 'tensor')
- down_grad: float32 [8192, 2048], P('tensor', 'dp')
- down_first_next: float32 [8192, 2048], P('tensor', 'dp')
- down_second_next: float32 [8192, 2048], P('tensor', 'dp')
- down_master: float32 [8192, 2048], P('tensor', 'dp')
Inputs may be any that keep to these rules, and one draw needn't show every extreme that they name: Each row of 6 lengths sums to 1536 and its largest is exactly 1024. `places`: each row names every place of its group once. `owners`: each row names every block once.
All inputs are finite; a program needn't handle non-finite values.
Results may differ from a plain program's by a relative error of at most 0.02.
Values may be sent and summed in bfloat16 or wider, within the bound.
No kernel may reach another device: no remote copies, remote signals or barrier semaphores. Data moves between devices by JAX's collectives and lax.ppermute only.
A program may use at most 320 MiB of HBM per device.

v0:
```python
import math
import jax
import jax.numpy as jnp
from jax import lax
from jax.sharding import PartitionSpec as P

HD = 128
RATES = (0.03, 0.06, 0.02, 0.01)


def inverse_order(order):
    count = order.shape[0]
    return jnp.zeros((count,), jnp.int32).at[order].set(jnp.arange(count, dtype=jnp.int32))


def reorder_blocks(weight, order):
    shape = weight.shape
    split = shape[:1] + (order.shape[0], shape[1] // order.shape[0]) + shape[2:]
    return jnp.take(weight.reshape(split), order, axis=1).reshape(shape)


def normalize(values):
    center = values - jnp.mean(values, axis=-1, keepdims=True)
    scale = lax.rsqrt(jnp.mean(center * center, axis=-1, keepdims=True) + 1e-05)
    return (center * scale, scale)


def normalize_back(normed, scale, grad):
    return scale * (
        grad
        - jnp.mean(grad, axis=-1, keepdims=True)
        - normed * jnp.mean(grad * normed, axis=-1, keepdims=True)
    )


def rotate(values, cosine, sine):
    half = values.shape[-1] // 2
    first = values[..., :half]
    second = values[..., half:]
    return jnp.concatenate(
        [first * cosine - second * sine, second * cosine + first * sine], axis=-1
    )


def rotate_back(grad, cosine, sine):
    half = grad.shape[-1] // 2
    first = grad[..., :half]
    second = grad[..., half:]
    return jnp.concatenate(
        [first * cosine + second * sine, second * cosine - first * sine], axis=-1
    )


def layout(lengths, count, head_size):
    place = jnp.arange(count, dtype=jnp.int32)
    ends = jnp.cumsum(lengths)
    starts = ends - lengths
    segment = jnp.sum((place[:, None] >= ends[None, :]).astype(jnp.int32), axis=1)
    begin = jnp.max(jnp.where(starts[None, :] <= place[:, None], starts[None, :], 0), axis=1)
    position = (place - begin).astype(jnp.float32)
    half = head_size // 2
    freq = jnp.exp(jnp.arange(half, dtype=jnp.float32) * (-2.0 * math.log(10000.0) / head_size))
    angle = position[:, None] * freq[None, :]
    return (segment, place, jnp.cos(angle), jnp.sin(angle))


def block_scores(query_block, keys, segment, place, start, width):
    finish = start + width
    scores = jnp.einsum(
        "hqd,hkd->hqk", query_block, keys[:, :finish], preferred_element_type=jnp.float32
    ) * keys.shape[-1] ** (-0.5)
    allowed = (segment[start:finish][:, None] == segment[None, :finish]) & (
        place[None, :finish] <= place[start:finish][:, None]
    )
    return jnp.where(allowed[None], scores, -1e30)


def gather_normed(rows):
    return lax.all_gather(rows, "tensor", axis=0, tiled=True)


def gather_grads(rows):
    return lax.all_gather(rows, "tensor", axis=0, tiled=True)


def sum_branch(partial_rows):
    return lax.psum_scatter(
        partial_rows.astype(jnp.bfloat16), "tensor", scatter_dimension=0, tiled=True
    ).astype(jnp.float32)


def sum_inputs(partial_rows):
    return lax.psum_scatter(
        partial_rows.astype(jnp.bfloat16), "tensor", scatter_dimension=0, tiled=True
    ).astype(jnp.float32)


def reduce_owned(terms, owners):
    return (
        lax.psum_scatter(
            reorder_blocks(terms[0], owners[0]).astype(jnp.bfloat16),
            "dp",
            scatter_dimension=1,
            tiled=True,
        ).astype(jnp.float32),
        lax.psum_scatter(
            reorder_blocks(terms[1], owners[1]).astype(jnp.bfloat16),
            "dp",
            scatter_dimension=1,
            tiled=True,
        ).astype(jnp.float32),
        lax.psum_scatter(
            reorder_blocks(terms[2], owners[2]).astype(jnp.bfloat16),
            "dp",
            scatter_dimension=1,
            tiled=True,
        ).astype(jnp.float32),
        lax.psum_scatter(
            reorder_blocks(terms[3], owners[3]).astype(jnp.bfloat16),
            "dp",
            scatter_dimension=1,
            tiled=True,
        ).astype(jnp.float32),
    )


def adamw(master, first, second, grad, rate):
    first_next = 0.5 * first + 0.5 * grad
    second_next = 0.5 * second + 0.5 * grad * grad
    master_next = master - rate * (first_next / (jnp.sqrt(second_next) + 1e-08) + 0.1 * master)
    return (grad, first_next, second_next, master_next)


def body(
    tokens,
    cotangent,
    lengths,
    places,
    owners,
    qkv_weight,
    qkv_first,
    qkv_second,
    out_weight,
    out_first,
    out_second,
    proj_weight,
    proj_first,
    proj_second,
    down_weight,
    down_first,
    down_second,
):
    fetched = (
        lax.all_gather(qkv_weight.astype(jnp.bfloat16), "dp", axis=1, tiled=True),
        lax.all_gather(out_weight.astype(jnp.bfloat16), "dp", axis=1, tiled=True),
        lax.all_gather(proj_weight.astype(jnp.bfloat16), "dp", axis=1, tiled=True),
        lax.all_gather(down_weight.astype(jnp.bfloat16), "dp", axis=1, tiled=True),
    )
    w_qkv = reorder_blocks(fetched[0], inverse_order(owners[0]))
    w_out = reorder_blocks(fetched[1], inverse_order(owners[1]))
    w_proj = reorder_blocks(fetched[2], inverse_order(owners[2]))
    w_down = reorder_blocks(fetched[3], inverse_order(owners[3]))
    local_cols = w_qkv.shape[2]
    local_heads = local_cols // HD
    group_rows = places.shape[2]
    width = min(512, group_rows)
    scale = HD ** (-0.5)
    logical = (
        jnp.zeros(w_qkv.shape, jnp.float32),
        jnp.zeros(w_out.shape, jnp.float32),
        jnp.zeros(w_proj.shape, jnp.float32),
        jnp.zeros(w_down.shape, jnp.float32),
    )
    owned = (
        jnp.zeros(qkv_weight.shape, jnp.float32),
        jnp.zeros(out_weight.shape, jnp.float32),
        jnp.zeros(proj_weight.shape, jnp.float32),
        jnp.zeros(down_weight.shape, jnp.float32),
    )
    outputs = []
    input_grads = []
    for micro_batch in range(tokens.shape[0]):
        order = places[micro_batch, 0]
        back = inverse_order(order)
        segment, place, cosine, sine = layout(lengths[micro_batch, 0], group_rows, HD)
        rows_in = tokens[micro_batch].astype(jnp.float32)
        normed_one, scale_one = normalize(rows_in)
        rows_a = gather_normed(normed_one.astype(jnp.bfloat16))[order]
        joined = jnp.einsum("td,sdc->stc", rows_a, w_qkv, preferred_element_type=jnp.float32)
        heads = joined.reshape(3, group_rows, local_heads, HD).transpose(0, 2, 1, 3)
        query = rotate(heads[0], cosine, sine).astype(jnp.bfloat16)
        keys = rotate(heads[1], cosine, sine).astype(jnp.bfloat16)
        values = heads[2].astype(jnp.bfloat16)
        pieces = []
        lse_list = []
        for start in range(0, group_rows, width):
            finish = start + width
            scores = block_scores(query[:, start:finish], keys, segment, place, start, width)
            top = jnp.max(scores, axis=-1, keepdims=True)
            expo = jnp.exp(scores - top)
            total = jnp.sum(expo, axis=-1, keepdims=True)
            probs = expo / total
            lse_list.append(top + jnp.log(total))
            pieces.append(
                jnp.einsum(
                    "hqk,hkd->hqd",
                    probs.astype(jnp.bfloat16),
                    values[:, :finish],
                    preferred_element_type=jnp.float32,
                )
            )
        attended = jnp.concatenate(pieces, axis=1).astype(jnp.bfloat16)
        attn_rows = attended.transpose(1, 0, 2).reshape(group_rows, local_cols)
        branch_one = sum_branch(jnp.dot(attn_rows, w_out, preferred_element_type=jnp.float32)[back])
        middle = rows_in + branch_one
        normed_two, scale_two = normalize(middle)
        rows_b = gather_normed(normed_two.astype(jnp.bfloat16))
        gate_up = jnp.einsum("td,sdf->stf", rows_b, w_proj, preferred_element_type=jnp.float32)
        sigma = jax.nn.sigmoid(gate_up[0])
        activated = gate_up[0] * sigma
        hidden = (activated * gate_up[1]).astype(jnp.bfloat16)
        branch_two = sum_branch(jnp.dot(hidden, w_down, preferred_element_type=jnp.float32))
        outputs.append((middle + branch_two).astype(jnp.bfloat16))
        grad_out = cotangent[micro_batch].astype(jnp.float32)
        grads_two = gather_grads(grad_out.astype(jnp.bfloat16))
        term_down = jnp.einsum("tf,td->fd", hidden, grads_two, preferred_element_type=jnp.float32)
        grad_hidden = jnp.einsum("td,fd->tf", grads_two, w_down, preferred_element_type=jnp.float32)
        grad_gate = grad_hidden * gate_up[1] * sigma * (1.0 + gate_up[0] * (1.0 - sigma))
        grad_up = grad_hidden * activated
        grad_gate_up = jnp.stack([grad_gate, grad_up]).astype(jnp.bfloat16)
        term_proj = jnp.einsum(
            "td,stf->sdf", rows_b, grad_gate_up, preferred_element_type=jnp.float32
        )
        grad_normed_two = sum_inputs(
            jnp.einsum("stf,sdf->td", grad_gate_up, w_proj, preferred_element_type=jnp.float32)
        )
        grad_middle = grad_out + normalize_back(normed_two, scale_two, grad_normed_two)
        grads_one = gather_grads(grad_middle.astype(jnp.bfloat16))[order]
        term_out = jnp.einsum("tc,td->cd", attn_rows, grads_one, preferred_element_type=jnp.float32)
        grad_attn = jnp.einsum(
            "td,cd->tc", grads_one, w_out, preferred_element_type=jnp.float32
        ).astype(jnp.bfloat16)
        grad_heads = grad_attn.reshape(group_rows, local_heads, HD).transpose(1, 0, 2)
        grad_query_list = []
        grad_keys = jnp.zeros(keys.shape, jnp.float32)
        grad_values = jnp.zeros(values.shape, jnp.float32)
        for number, start in enumerate(range(0, group_rows, width)):
            finish = start + width
            query_block = query[:, start:finish]
            grad_block = grad_heads[:, start:finish]
            scores = block_scores(query_block, keys, segment, place, start, width)
            probs = jnp.exp(scores - lse_list[number])
            grad_probs = jnp.einsum(
                "hqd,hkd->hqk", grad_block, values[:, :finish], preferred_element_type=jnp.float32
            )
            delta = jnp.sum(grad_probs * probs, axis=-1, keepdims=True)
            grad_scores = (probs * (grad_probs - delta)).astype(jnp.bfloat16)
            grad_query_list.append(
                jnp.einsum(
                    "hqk,hkd->hqd",
                    grad_scores,
                    keys[:, :finish],
                    preferred_element_type=jnp.float32,
                )
                * scale
            )
            grad_keys = grad_keys.at[:, :finish].add(
                jnp.einsum(
                    "hqk,hqd->hkd", grad_scores, query_block, preferred_element_type=jnp.float32
                )
                * scale
            )
            grad_values = grad_values.at[:, :finish].add(
                jnp.einsum(
                    "hqk,hqd->hkd",
                    probs.astype(jnp.bfloat16),
                    grad_block,
                    preferred_element_type=jnp.float32,
                )
            )
        grad_query = rotate_back(jnp.concatenate(grad_query_list, axis=1), cosine, sine)
        grad_keys = rotate_back(grad_keys, cosine, sine)
        grad_joined = jnp.stack([grad_query, grad_keys, grad_values]).astype(jnp.bfloat16)
        grad_joined = grad_joined.transpose(0, 2, 1, 3).reshape(3, group_rows, local_cols)
        term_qkv = jnp.einsum(
            "td,stc->sdc", rows_a, grad_joined, preferred_element_type=jnp.float32
        )
        grad_normed_one = sum_inputs(
            jnp.einsum("stc,sdc->td", grad_joined, w_qkv, preferred_element_type=jnp.float32)[back]
        )
        input_grads.append(grad_middle + normalize_back(normed_one, scale_one, grad_normed_one))
        terms = (term_qkv, term_out, term_proj, term_down)
        logical = tuple((running + current for running, current in zip(logical, terms)))
    owned = reduce_owned(logical, owners)
    qkv_new = adamw(qkv_weight, qkv_first, qkv_second, owned[0], RATES[0])
    out_new = adamw(out_weight, out_first, out_second, owned[1], RATES[1])
    proj_new = adamw(proj_weight, proj_first, proj_second, owned[2], RATES[2])
    down_new = adamw(down_weight, down_first, down_second, owned[3], RATES[3])
    return (
        jnp.stack(outputs),
        jnp.stack(input_grads),
        qkv_new[0],
        qkv_new[1],
        qkv_new[2],
        qkv_new[3],
        out_new[0],
        out_new[1],
        out_new[2],
        out_new[3],
        proj_new[0],
        proj_new[1],
        proj_new[2],
        proj_new[3],
        down_new[0],
        down_new[1],
        down_new[2],
        down_new[3],
    )


def solution(mesh):
    placed = (
        P(None, ("dp", "tensor"), None),
        P(None, ("dp", "tensor"), None),
        P(None, "dp", None),
        P(None, "dp", None),
        P(),
        P(None, "dp", "tensor"),
        P(None, "dp", "tensor"),
        P(None, "dp", "tensor"),
        P("tensor", "dp"),
        P("tensor", "dp"),
        P("tensor", "dp"),
        P(None, "dp", "tensor"),
        P(None, "dp", "tensor"),
        P(None, "dp", "tensor"),
        P("tensor", "dp"),
        P("tensor", "dp"),
        P("tensor", "dp"),
    )
    return jax.shard_map(
        body,
        mesh=mesh,
        in_specs=placed,
        out_specs=(
            P(None, ("dp", "tensor"), None),
            P(None, ("dp", "tensor"), None),
            P(None, "dp", "tensor"),
            P(None, "dp", "tensor"),
            P(None, "dp", "tensor"),
            P(None, "dp", "tensor"),
            P("tensor", "dp"),
            P("tensor", "dp"),
            P("tensor", "dp"),
            P("tensor", "dp"),
            P(None, "dp", "tensor"),
            P(None, "dp", "tensor"),
            P(None, "dp", "tensor"),
            P(None, "dp", "tensor"),
            P("tensor", "dp"),
            P("tensor", "dp"),
            P("tensor", "dp"),
            P("tensor", "dp"),
        ),
        check_vma=False,
    )
```

profile of v0, /device:TPU:0, one launch (start us, length us, event | category | flops | bytes accessed | tf_op | source)
XLA Modules:
  0.0 1725.9 jit_solution(1794120397904735243)
XLA Ops:
  48.3 38.6 %all-gather.15.cloned.1.call-done = bf16[3,2048,256]{2,1,0:T(8,128)(2,1)} async-done(((bf16[3,512,256]{2,1,0:T(8,128)(2,1)}), bf16[3,2048,256]{2,1,0:T(8,128)(2,1)}) %all-gather.15.cloned.1.call-update) | async-done | bytes 3145744 | tf_op jit(solution)/shard_map/all_gather | solution.py:154
  95.4 58.4 %all-gather.17.cloned.1.call-done = bf16[1536,2048]{1,0:T(8,128)(2,1)} async-done(((bf16[192,2048]{1,0:T(8,128)(2,1)}), bf16[1536,2048]{1,0:T(8,128)(2,1)}) %all-gather.17.cloned.1.call-update) | async-done | bytes 6291472 | tf_op jit(solution)/shard_map/all_gather | solution.py:79
  153.9 16.3 gather_fusion.1
  170.1 9.6 fusion.39
  213.5 16.3 gather_fusion.3
  236.9 61.5 %reduce-scatter.13.cloned.1.call-done = bf16[192,2048]{1,0:T(8,128)(2,1)} async-done(((bf16[1536,2048]{1,0:T(8,128)(2,1)}), bf16[192,2048]{1,0:T(8,128)(2,1)}) %reduce-scatter.13.cloned.1.call-update) | async-done | bytes 786448 | tf_op jit(solution)/shard_map/reduce_scatter | solution.py:87
  306.9 44.8 %all-gather.25.cloned.1.call-done = bf16[1024,2048]{1,0:T(8,128)(2,1)} async-done(((bf16[1024,512]{1,0:T(8,128)(2,1)}), bf16[1024,2048]{1,0:T(8,128)(2,1)}) %all-gather.25.cloned.1.call-update) | async-done | bytes 4194320 | tf_op jit(solution)/shard_map/all_gather | solution.py:157
  368.4 73.0 %all-gather.21.cloned.1.call-done = bf16[2,2048,1024]{2,1,0:T(8,128)(2,1)} async-done(((bf16[2,512,1024]{2,1,0:T(8,128)(2,1)}), bf16[2,2048,1024]{2,1,0:T(8,128)(2,1)}) %all-gather.21.cloned.1.call-update) | async-done | bytes 8388624 | tf_op jit(solution)/shard_map/all_gather | solution.py:156
  457.5 7.9 pad_maximum_fusion.1
  480.8 27.6 %all-gather.23.cloned.1.call-done = bf16[1536,2048]{1,0:T(8,128)(2,1)} async-done(((bf16[192,2048]{1,0:T(8,128)(2,1)}), bf16[1536,2048]{1,0:T(8,128)(2,1)}) %all-gather.23.cloned.1.call-update) | async-done | bytes 6291472 | tf_op jit(solution)/shard_map/all_gather | solution.py:79
  508.3 19.2 %convolution_bitcast_fusion.3 = f32[2,1536,1024]{1,2,0:T(8,128)} fusion(bf16[2,2048,1024]{2,1,0:T(8,128)(2,1)} %bitcast_select_fusion.1, bf16[1536,2048]{1,0:T(8,128)(2,1)} %all-gather.23.cloned.1.call-done), kind=kOutput, calls=%fused_computation.38 | convolution fusion | flops 12884901888 | bytes 27262976 | tf_op jit(solution)/shard_map/td,sdf->stf/dot_general | solution.py:218
  527.5 14.3 convolution_convert_fusion.1
  546.3 27.0 %all-gather.35.cloned.1.call-done = bf16[1,1536,2048]{2,1,0:T(8,128)(2,1)} async-done(((bf16[1,192,2048]{2,1,0:T(8,128)(2,1)}), bf16[1,1536,2048]{2,1,0:T(8,128)(2,1)}) %all-gather.35.cloned.1.call-update) | async-done | bytes 6291472 | tf_op jit(solution)/shard_map/all_gather | solution.py:83
  573.3 14.9 fusion.71
  590.9 17.7 %bitcast_convert_fusion.1 = bf16[1536,2048]{1,0:T(8,128)(2,1)} fusion(bf16[2,2048,1024]{2,1,0:T(8,128)(2,1)} %bitcast_select_fusion.1, bf16[1,1536,1024]{1,2,0:T(8,128)(2,1)S(1)} %get-tuple-element.266, bf16[1,1536,1024]{1,2,0:T(8,128)(2,1)S(1)} %get-tuple-element.265), kind=kOutput, calls=%fused_computation.29 | convolution fusion | flops 12891193344 | bytes 20971520 | tf_op jit(solution)/shard_map/stf,sdf->td/dot_general | solution.py:235
  609.2 34.9 %reduce-scatter.15.cloned.1.call-done = bf16[192,2048]{1,0:T(8,128)(2,1)} async-done(((bf16[1536,2048]{1,0:T(8,128)(2,1)}), bf16[192,2048]{1,0:T(8,128)(2,1)}) %reduce-scatter.15.cloned.1.call-update) | async-done | bytes 786448 | tf_op jit(solution)/shard_map/reduce_scatter | solution.py:87
  644.1 70.4 %reduce-scatter.21.cloned.1.call-done = bf16[192,2048]{1,0:T(8,128)(2,1)} async-done(((bf16[1536,2048]{1,0:T(8,128)(2,1)}), bf16[192,2048]{1,0:T(8,128)(2,1)}) %reduce-scatter.21.cloned.1.call-update) | async-done | bytes 786448 | tf_op jit(solution)/shard_map/reduce_scatter | solution.py:93
  727.3 56.4 %all-gather.27.cloned.1.call-done = bf16[1536,2048]{1,0:T(8,128)(2,1)} async-done(((bf16[192,2048]{1,0:T(8,128)(2,1)}), bf16[1536,2048]{1,0:T(8,128)(2,1)}) %all-gather.27.cloned.1.call-update) | async-done | bytes 6291472 | tf_op jit(solution)/shard_map/all_gather | solution.py:79
  783.7 16.3 gather_fusion.5
  800.0 9.7 fusion.32
  838.1 16.3 gather_fusion.6
  857.0 17.1 gather_fusion.7
  907.0 9.6 convolution_bitcast_fusion.1
  916.7 16.4 gather_fusion.8
  933.2 68.0 %reduce-scatter.23.cloned.1.call-done = bf16[192,2048]{1,0:T(8,128)(2,1)} async-done(((bf16[1536,2048]{1,0:T(8,128)(2,1)}), bf16[192,2048]{1,0:T(8,128)(2,1)}) %reduce-scatter.23.cloned.1.call-update) | async-done | bytes 786448 | tf_op jit(solution)/shard_map/reduce_scatter | solution.py:93
  1006.1 62.7 %all-gather.29.cloned.1.call-done = bf16[1536,2048]{1,0:T(8,128)(2,1)} async-done(((bf16[192,2048]{1,0:T(8,128)(2,1)}), bf16[1536,2048]{1,0:T(8,128)(2,1)}) %all-gather.29.cloned.1.call-update) | async-done | bytes 6291472 | tf_op jit(solution)/shard_map/all_gather | solution.py:79
  1068.8 19.2 %convolution_bitcast_fusion.2 = f32[2,1536,1024]{1,2,0:T(8,128)} fusion(bf16[2,2048,1024]{2,1,0:T(8,128)(2,1)} %bitcast_select_fusion.1, bf16[1536,2048]{1,0:T(8,128)(2,1)} %all-gather.29.cloned.1.call-done), kind=kOutput, calls=%fused_computation.37 | convolution fusion | flops 12884901888 | bytes 27262976 | tf_op jit(solution)/shard_map/td,sdf->stf/dot_general | solution.py:218
  1088.0 46.2 %all-gather.37.cloned.1.call-done = bf16[1,1536,2048]{2,1,0:T(8,128)(2,1)} async-done(((bf16[1,192,2048]{2,1,0:T(8,128)(2,1)}), bf16[1,1536,2048]{2,1,0:T(8,128)(2,1)}) %all-gather.37.cloned.1.call-update) | async-done | bytes 6291472 | tf_op jit(solution)/shard_map/all_gather | solution.py:83
  1134.2 15.1 fusion.72
  1151.9 17.8 %bitcast_convert_fusion = bf16[1536,2048]{1,0:T(8,128)(2,1)} fusion(bf16[2,2048,1024]{2,1,0:T(8,128)(2,1)} %bitcast_select_fusion.1, bf16[1,1536,1024]{1,2,0:T(8,128)(2,1)S(1)} %get-tuple-element.264, bf16[1,1536,1024]{1,2,0:T(8,128)(2,1)S(1)} %get-tuple-element.263), kind=kOutput, calls=%fused_computation.28 | convolution fusion | flops 12891193344 | bytes 20971520 | tf_op jit(solution)/shard_map/stf,sdf->td/dot_general | solution.py:235
  1169.8 15.1 convolution_convert_fusion
  1185.4 52.9 %reduce-scatter.25.cloned.1.call-done = bf16[192,2048]{1,0:T(8,128)(2,1)} async-done(((bf16[1536,2048]{1,0:T(8,128)(2,1)}), bf16[192,2048]{1,0:T(8,128)(2,1)}) %reduce-scatter.25.cloned.1.call-update) | async-done | bytes 786448 | tf_op jit(solution)/shard_map/reduce_scatter | solution.py:93
  1240.1 68.5 %reduce-scatter.19.cloned.1.call-done = bf16[192,2048]{1,0:T(8,128)(2,1)} async-done(((bf16[1536,2048]{1,0:T(8,128)(2,1)}), bf16[192,2048]{1,0:T(8,128)(2,1)}) %reduce-scatter.19.cloned.1.call-update) | async-done | bytes 786448 | tf_op jit(solution)/shard_map/reduce_scatter | solution.py:87
  1313.2 11.7 fusion.11
  1324.9 13.1 fusion.46
  1363.2 19.6 %fusion.34 = f32[2,1024,2048]{2,1,0:T(8,128)} fusion(bf16[1536,2048]{1,0:T(8,128)(2,1)} %all-gather.23.cloned.1.call-done, bf16[1,1536,1024]{1,2,0:T(8,128)(2,1)} %copy-done.149, bf16[1,1536,1024]{1,2,0:T(8,128)(2,1)S(1)} %copy-done.148), kind=kOutput, calls=%fused_computation.87 | convolution fusion | flops 12888047616 | bytes 29360128 | tf_op jit(solution)/shard_map/td,stf->sdf/dot_general | solution.py:231
  1382.8 22.3 %add_bitcast_fusion = bf16[2,2048,1024]{1,2,0:T(8,128)(2,1)} fusion(f32[2,1024,2048]{2,1,0:T(8,128)} %fusion.34, bf16[1536,2048]{1,0:T(8,128)(2,1)} %all-gather.29.cloned.1.call-done, bf16[1,1536,1024]{1,2,0:T(8,128)(2,1)} %copy-done.151, bf16[1,1536,1024]{1,2,0:T(8,128)(2,1)} %copy-done.150), kind=kOutput, calls=%fused_computation.27 | convolution fusion | flops 12896436224 | bytes 37748736 | tf_op jit(solution)/shard_map/td,stf->sdf/dot_general | solution.py:231
  1405.1 14.6 reshape.1437
  1419.7 8.2 fusion.251
  1453.0 7.9 pad_maximum_fusion
  1468.6 8.2 fusion
  1483.9 16.4 gather_fusion.9
  1554.9 9.3 add_bitcast_fusion.1
  1576.0 9.1 convolution_bitcast_fusion
  1585.1 16.5 gather_fusion.10
  1613.0 10.7 multiply_subtract_fusion
  1629.2 11.2 reduce-scatter.29.cloned.1.call-done
  1646.0 66.3 %reduce-scatter.27.cloned.1.call-done = bf16[192,2048]{1,0:T(8,128)(2,1)} async-done(((bf16[1536,2048]{1,0:T(8,128)(2,1)}), bf16[192,2048]{1,0:T(8,128)(2,1)}) %reduce-scatter.27.cloned.1.call-update) | async-done | bytes 786448 | tf_op jit(solution)/shard_map/reduce_scatter | solution.py:93
  (622 shorter events, 404.0 us)
Async XLA Ops:
  7.2 33.4 %all-gather.19.cloned.1.call-start = ((), (), s32[]{:S(2)}) async-start(), calls=%async_computation.14 | async-start | bytes 1310720 | tf_op jit(solution)/shard_map/all_gather | solution.py:155
  11.2 75.7 %all-gather.15.cloned.1.call-start = ((), (), s32[]{:S(2)}) async-start(), calls=%async_computation.12 | async-start | bytes 3932160 | tf_op jit(solution)/shard_map/all_gather | solution.py:154
  12.3 141.6 %all-gather.17.cloned.1.call-start = ((), (), s32[]{:S(2)}) async-start(), calls=%async_computation.13 | async-start | bytes 7077888 | tf_op jit(solution)/shard_map/all_gather | solution.py:79
  15.6 282.8 %reduce-scatter.13.cloned.1.call-start = ((), (), s32[]{:S(2)}) async-start(), calls=%async_computation.15 | async-start | bytes 7077888 | tf_op jit(solution)/shard_map/reduce_scatter | solution.py:87
  16.1 289.5 %copy-start.143 = (s32[4]{0:T(128)}, s32[4]{0:T(128)S(1)}, u32[]{:S(2)}) copy-start(s32[4]{0:T(128)S(1)} %get-tuple-element.328) | copy-start | bytes 52
  25.3 128.5 %copy-start.88 = (s32[2048]{0:T(1024)}, s32[2048]{0:T(1024)S(1)}, u32[]{:S(2)}) copy-start(s32[2048]{0:T(1024)S(1)} %pad_clamp_fusion.3) | copy-start | bytes 24580
  25.4 188.2 %copy-start.86 = (s32[2048]{0:T(1024)}, s32[2048]{0:T(1024)S(1)}, u32[]{:S(2)}) copy-start(s32[2048]{0:T(1024)S(1)} %pad_clamp_fusion.2) | copy-start | bytes 24580
  25.5 19.2 %copy-start.129 = (pred[4]{0:T(512)(128)(4,1)}, pred[4]{0:T(512)(128)(4,1)S(1)}, u32[]{:S(2)}) copy-start(pred[4]{0:T(512)(128)(4,1)S(1)} %get-tuple-element.362) | copy-start | bytes 16
  35.7 154.5 %copy-start.40 = (f32[1536,64]{1,0:T(8,128)}, f32[1536,64]{1,0:T(8,128)S(1)}, u32[]{:S(2)}) copy-start(f32[1536,64]{1,0:T(8,128)S(1)} %get-tuple-element.334) | copy-start | bytes 1179652
  48.3 160.6 %copy-start.31 = (bf16[256,4,512]{0,2,1:T(8,128)(2,1)}, bf16[256,4,512]{0,2,1:T(8,128)(2,1)S(1)}, u32[]{:S(2)}) copy-start(bf16[256,4,512]{0,2,1:T(8,128)(2,1)S(1)} %copy.218) | copy-start | bytes 3145732
  229.9 121.7 %all-gather.25.cloned.1.call-start = ((), (), s32[]{:S(2)}) async-start(), calls=%async_computation.18 | async-start | bytes 5242880 | tf_op jit(solution)/shard_map/all_gather | solution.py:157
  232.7 208.7 %all-gather.21.cloned.1.call-start = ((), (), s32[]{:S(2)}) async-start(), calls=%async_computation.16 | async-start | bytes 10485760 | tf_op jit(solution)/shard_map/all_gather | solution.py:156
  236.9 271.4 %all-gather.23.cloned.1.call-start = ((), (), s32[]{:S(2)}) async-start(), calls=%async_computation.17 | async-start | bytes 7077888 | tf_op jit(solution)/shard_map/all_gather | solution.py:79
  302.7 270.7 %all-gather.35.cloned.1.call-start = ((), (), s32[]{:S(2)}) async-start(), calls=%async_computation.34 | async-start | bytes 7077888 | tf_op jit(solution)/shard_map/all_gather | solution.py:83
  305.5 338.6 %reduce-scatter.15.cloned.1.call-start = ((), (), s32[]{:S(2)}) async-start(), calls=%async_computation.19 | async-start | bytes 7077888 | tf_op jit(solution)/shard_map/reduce_scatter | solution.py:87
  541.9 172.6 %reduce-scatter.21.cloned.1.call-start = ((), (), s32[]{:S(2)}) async-start(), calls=%async_computation.24 | async-start | bytes 7077888 | tf_op jit(solution)/shard_map/reduce_scatter | solution.py:93
  608.6 175.1 %all-gather.27.cloned.1.call-start = ((), (), s32[]{:S(2)}) async-start(), calls=%async_computation.20 | async-start | bytes 7077888 | tf_op jit(solution)/shard_map/all_gather | solution.py:79
  609.2 111.1 %copy-start.108 = (f32[192]{0:T(256)}, f32[192]{0:T(256)S(1)}, u32[]{:S(2)}) copy-start(f32[192]{0:T(256)S(1)} %broadcast_multiply_fusion.9) | copy-start | bytes 2308
  720.4 136.6 %all-gather.31.cloned.1.call-start = ((), (), s32[]{:S(2)}) async-start(), calls=%async_computation.25 | async-start | bytes 7077888 | tf_op jit(solution)/shard_map/all_gather | solution.py:83
  721.0 212.2 %reduce-scatter.17.cloned.1.call-start = ((), (), s32[]{:S(2)}) async-start(), calls=%async_computation.21 | async-start | bytes 7077888 | tf_op jit(solution)/shard_map/reduce_scatter | solution.py:87
  727.2 72.8 %copy-start.90 = (s32[2048]{0:T(1024)}, s32[2048]{0:T(1024)S(1)}, u32[]{:S(2)}) copy-start(s32[2048]{0:T(1024)S(1)} %pad_clamp_fusion.1) | copy-start | bytes 24580
  727.3 110.8 %copy-start.84 = (s32[2048]{0:T(1024)}, s32[2048]{0:T(1024)S(1)}, u32[]{:S(2)}) copy-start(s32[2048]{0:T(1024)S(1)} %pad_clamp_fusion) | copy-start | bytes 24580
  727.3 72.7 %copy-start.55 = (bf16[3,2048,256]{2,1,0:T(8,128)(2,1)S(1)}, bf16[3,2048,256]{2,1,0:T(8,128)(2,1)}, u32[]{:S(2)}) copy-start(bf16[3,2048,256]{2,1,0:T(8,128)(2,1)} %bitcast_select_fusion.5) | copy-start | bytes 9437188
  854.5 146.7 %reduce-scatter.23.cloned.1.call-start = ((), (), s32[]{:S(2)}) async-start(), calls=%async_computation.26 | async-start | bytes 7077888 | tf_op jit(solution)/shard_map/reduce_scatter | solution.py:93
  933.1 68.1 %copy-start.1 = (bf16[2,192,2048]{2,1,0:T(8,128)(2,1)S(1)}, bf16[2,192,2048]{2,1,0:T(8,128)(2,1)}, u32[]{:S(2)}) copy-start(bf16[2,192,2048]{2,1,0:T(8,128)(2,1)} %param.49) | copy-start | bytes 4718596
  933.1 68.1 %copy-start.106 = (f32[192]{0:T(256)S(1)}, f32[192]{0:T(256)}, u32[]{:S(2)}) copy-start(f32[192]{0:T(256)} %copy-done.105) | copy-start | bytes 2308
  933.1 68.1 %copy-start.123 = (f32[192]{0:T(256)S(1)}, f32[192]{0:T(256)}, u32[]{:S(2)}) copy-start(f32[192]{0:T(256)} %copy-done.122) | copy-start | bytes 2308
  933.1 135.7 %all-gather.29.cloned.1.call-start = ((), (), s32[]{:S(2)}) async-start(), calls=%async_computation.22 | async-start | bytes 7077888 | tf_op jit(solution)/shard_map/all_gather | solution.py:79
  933.2 70.7 %copy-start.30 = (bf16[192,2048]{1,0:T(8,128)(2,1)S(1)}, bf16[192,2048]{1,0:T(8,128)(2,1)}, u32[]{:S(2)}) copy-start(bf16[192,2048]{1,0:T(8,128)(2,1)} %reduce-scatter.17.cloned.1.call-done) | copy-start | bytes 2359300
  1005.5 128.8 %all-gather.37.cloned.1.call-start = ((), (), s32[]{:S(2)}) async-start(), calls=%async_computation.35 | async-start | bytes 7077888 | tf_op jit(solution)/shard_map/all_gather | solution.py:83
  1006.0 232.2 %reduce-scatter.25.cloned.1.call-start = ((), (), s32[]{:S(2)}) async-start(), calls=%async_computation.27 | async-start | bytes 7077888 | tf_op jit(solution)/shard_map/reduce_scatter | solution.py:93
  1169.8 138.9 %reduce-scatter.19.cloned.1.call-start = ((), (), s32[]{:S(2)}) async-start(), calls=%async_computation.23 | async-start | bytes 7077888 | tf_op jit(solution)/shard_map/reduce_scatter | solution.py:87
  1185.0 299.0 %all-gather.33.cloned.1.call-start = ((), (), s32[]{:S(2)}) async-start(), calls=%async_computation.28 | async-start | bytes 7077888 | tf_op jit(solution)/shard_map/all_gather | solution.py:83
  1240.1 72.9 %copy-start.138 = (pred[4]{0:T(512)(128)(4,1)S(1)}, pred[4]{0:T(512)(128)(4,1)}, u32[]{:S(2)}) copy-start(pred[4]{0:T(512)(128)(4,1)} %get-tuple-element.318) | copy-start | bytes 16
  1240.1 73.0 %copy-start.137 = (pred[4]{0:T(512)(128)(4,1)S(1)}, pred[4]{0:T(512)(128)(4,1)}, u32[]{:S(2)}) copy-start(pred[4]{0:T(512)(128)(4,1)} %get-tuple-element.321) | copy-start | bytes 16
  1240.1 73.1 %copy-start.144 = (s32[4]{0:T(128)S(1)}, s32[4]{0:T(128)}, u32[]{:S(2)}) copy-start(s32[4]{0:T(128)} %copy-done.143) | copy-start | bytes 52
  1240.1 73.0 %copy-start.146 = (s32[4]{0:T(128)S(1)}, s32[4]{0:T(128)}, u32[]{:S(2)}) copy-start(s32[4]{0:T(128)} %copy-done.145) | copy-start | bytes 52
  1312.9 292.0 %reduce-scatter.35.cloned.1.call-start = ((), (), s32[]{:S(2)}) async-start(), calls=%async_computation.33 | async-start | bytes 5242880 | tf_op jit(solution)/shard_map/reduce_scatter | solution.py:118
  1361.3 251.7 %reduce-scatter.33.cloned.1.call-start = ((), (), s32[]{:S(2)}) async-start(), calls=%async_computation.32 | async-start | bytes 10485760 | tf_op jit(solution)/shard_map/reduce_scatter | solution.py:112
  1476.9 146.9 %reduce-scatter.31.cloned.1.call-start = ((), (), s32[]{:S(2)}) async-start(), calls=%async_computation.31 | async-start | bytes 1310720 | tf_op jit(solution)/shard_map/reduce_scatter | solution.py:106
  1546.6 93.8 %reduce-scatter.29.cloned.1.call-start = ((), (), s32[]{:S(2)}) async-start(), calls=%async_computation.30 | async-start | bytes 3932160 | tf_op jit(solution)/shard_map/reduce_scatter | solution.py:100
  1574.2 138.1 %reduce-scatter.27.cloned.1.call-start = ((), (), s32[]{:S(2)}) async-start(), calls=%async_computation.29 | async-start | bytes 7077888 | tf_op jit(solution)/shard_map/reduce_scatter | solution.py:93
  1629.1 83.1 %copy-start.2 = (bf16[2,192,2048]{2,1,0:T(8,128)(2,1)S(1)}, bf16[2,192,2048]{2,1,0:T(8,128)(2,1)}, u32[]{:S(2)}) copy-start(bf16[2,192,2048]{2,1,0:T(8,128)(2,1)} %param.49) | copy-start | bytes 4718596
  1629.1 83.1 %copy-start.109 = (f32[192]{0:T(256)S(1)}, f32[192]{0:T(256)}, u32[]{:S(2)}) copy-start(f32[192]{0:T(256)} %copy-done.108) | copy-start | bytes 2308
  1629.1 83.1 %copy-start.126 = (f32[192]{0:T(256)S(1)}, f32[192]{0:T(256)}, u32[]{:S(2)}) copy-start(f32[192]{0:T(256)} %copy-done.125) | copy-start | bytes 2308
  1629.1 84.8 %copy-start.45 = (f32[192,2048]{1,0:T(8,128)S(1)}, f32[192,2048]{1,0:T(8,128)}, u32[]{:S(2)}) copy-start(f32[192,2048]{1,0:T(8,128)} %get-tuple-element.262) | copy-start | bytes 4718596
  1629.1 84.8 %copy-start.107 = (f32[192]{0:T(256)S(1)}, f32[192]{0:T(256)}, u32[]{:S(2)}) copy-start(f32[192]{0:T(256)} %copy-done.105) | copy-start | bytes 2308
  1629.2 84.8 %copy-start.124 = (f32[192]{0:T(256)S(1)}, f32[192]{0:T(256)}, u32[]{:S(2)}) copy-start(f32[192]{0:T(256)} %copy-done.122) | copy-start | bytes 2308
  (134 other events, 455.4 us)
Sparse Core Ops, SparseCore 0:
  11.4 29.2 all-gather.18
  43.0 43.8 all-gather.14
  89.1 64.6 all-gather.16
  230.0 68.3 reduce-scatter.12
  300.7 50.8 all-gather.24
  353.9 87.4 all-gather.20
  443.6 64.6 all-gather.22
  510.0 63.3 all-gather.34
  575.6 68.3 reduce-scatter.14
  646.2 68.1 reduce-scatter.20
  720.5 63.1 all-gather.26
  785.7 63.3 all-gather.30
  854.5 68.4 reduce-scatter.16
  933.2 67.9 reduce-scatter.22
  1005.6 63.1 all-gather.28
  1070.8 63.3 all-gather.36
  1169.9 68.3 reduce-scatter.24
  1240.4 68.1 reduce-scatter.18
  1313.1 63.1 all-gather.32
  1379.1 51.2 reduce-scatter.34
  1477.0 84.8 reduce-scatter.32
  1565.4 27.9 reduce-scatter.30
  1596.4 43.9 reduce-scatter.28
  1642.5 69.7 reduce-scatter.26
where the time goes:
time: 1730 us
  waiting for transfers between devices  872 us (50%)
  local copies, waits for them, and re-layouts  352 us (20%)
  matrix products  330 us (19%)
  other arithmetic  153 us (9%)
  between operations  17.3 us (1%)
    reduce_scatter x4, waiting for transfers between devices, sum_inputs(): lax.psum_scatter(partial_rows.astype(jnp.bfloat16), 'tensor', scatter_dim...  258 us
    all_gather x4, waiting for transfers between devices, gather_normed(): return lax.all_gather(rows, 'tensor', axis=0, tiled=True)  205 us
    reduce_scatter x4, waiting for transfers between devices, sum_branch(): lax.psum_scatter(partial_rows.astype(jnp.bfloat16), 'tensor', scatter_dim...  165 us
    all_gather x4, waiting for transfers between devices, gather_grads(): return lax.all_gather(rows, 'tensor', axis=0, tiled=True)  73.3 us
    all_gather x1, waiting for transfers between devices, body(): lax.all_gather(proj_weight.astype(jnp.bfloat16), 'dp', axis=1, tiled=True)  73 us
    gather x17, local copies, waits for them, and re-layouts, reorder_blocks(): return jnp.take(weight.reshape(split), order, axis=1).reshape(shape)  69.4 us
    unnamed x343, local copies, waits for them, and re-layouts  68.6 us
    all_gather x1, waiting for transfers between devices, body(): lax.all_gather(down_weight.astype(jnp.bfloat16), 'dp', axis=1, tiled=True)  44.8 us
  transfers between devices with their start and end apart: 24, of which 18 were waited for; matrix products, arithmetic and copies ran while one was open for 39% of the time, Pallas kernels for 0%

commit v1 on v0

--- a/solution.py
+++ b/solution.py
@@ -150,8 +150,24 @@
     down_first,
     down_second,
 ):
+
+    def group_run(in_array, at_axis):
+        mesh_ax = "dp"
+        s_next = lax.axis_size(mesh_ax)
+        latest = lax.axis_index(mesh_ax)
+        view_out, met_up, everything = (s_next, latest, in_array.shape[at_axis])
+        after, mixed_arr = (in_array, 1)
+        while mixed_arr < view_out:
+            val = range(view_out)
+            r_now = map(lambda m: (m, (m - mixed_arr) % view_out), val)
+            small = list(r_now)
+            current_block = lax.ppermute(after, axis_name=mesh_ax, perm=small)
+            after = jnp.concatenate([after, current_block], at_axis)
+            mixed_arr = 2 * mixed_arr
+        return jnp.roll(after, met_up * everything, at_axis)
+
     fetched = (
-        lax.all_gather(qkv_weight.astype(jnp.bfloat16), "dp", axis=1, tiled=True),
+        group_run(qkv_weight.astype(jnp.bfloat16), 1),
         lax.all_gather(out_weight.astype(jnp.bfloat16), "dp", axis=1, tiled=True),
         lax.all_gather(proj_weight.astype(jnp.bfloat16), "dp", axis=1, tiled=True),
         lax.all_gather(down_weight.astype(jnp.bfloat16), "dp", axis=1, tiled=True),

time: 1730 us -> 1710 us (0.988)
  waiting for transfers between devices: 872 us -> 827 us
    all_gather x1 -> x0, waiting for transfers between devices: 38.6 us -> none  [body(): lax.all_gather(qkv_weight.astype(jnp.bfloat16), 'dp', axis=1, tiled=True)]
    all_gather x4, waiting for transfers between devices: 205 us -> 178 us  [gather_normed(): return lax.all_gather(rows, 'tensor', axis=0, tiled=True)]
    unnamed x343 -> x353, local copies, waits for them, and re-layouts: 68.6 us -> 73.5 us
  transfers between devices with their start and end apart: 24 -> 25, of which waited for: 18 -> 19; matrix products, arithmetic and copies ran while one was open for 39% -> 41% of each run, Pallas kernels for 0% -> 0%
where the time goes in v1:
time: 1710 us; the launch traced here: 1700 us
  waiting for transfers between devices  827 us (48%)
  local copies, waits for them, and re-layouts  363 us (21%)
  matrix products  330 us (19%)
  other arithmetic  154 us (9%)
    reduce_scatter x4, waiting for transfers between devices, sum_inputs(): lax.psum_scatter(partial_rows.astype(jnp.bfloat16), 'tensor', scatter_dim...  258 us
    all_gather x4, waiting for transfers between devices, gather_normed(): return lax.all_gather(rows, 'tensor', axis=0, tiled=True)  178 us
    reduce_scatter x4, waiting for transfers between devices, sum_branch(): lax.psum_scatter(partial_rows.astype(jnp.bfloat16), 'tensor', scatter_dim...  165 us
    all_gather x4, waiting for transfers between devices, gather_grads(): return lax.all_gather(rows, 'tensor', axis=0, tiled=True)  73.5 us
    unnamed x353, local copies, waits for them, and re-layouts  73.5 us
    all_gather x1, waiting for transfers between devices, body(): lax.all_gather(proj_weight.astype(jnp.bfloat16), 'dp', axis=1, tiled=True)  73 us
    gather x17, local copies, waits for them, and re-layouts, reorder_blocks(): return jnp.take(weight.reshape(split), order, axis=1).reshape(shape)  69.5 us
    all_gather x1, waiting for transfers between devices, body(): lax.all_gather(down_weight.astype(jnp.bfloat16), 'dp', axis=1, tiled=True)  44.8 us
  transfers between devices with their start and end apart: 25, of which 19 were waited for; matrix products, arithmetic and copies ran while one was open for 41% of the time, Pallas kernels for 0%

profile of v1, /device:TPU:0, one launch (start us, length us, event | category | flops | bytes accessed | tf_op | source)
XLA Modules:
  0.0 1699.2 jit_solution(18264029920906282923)
XLA Ops:
  52.1 8.2 all-gather.16.cloned.1.call-done
  68.0 13.7 collective-permute-done.1
  101.5 25.8 %all-gather.14.cloned.1.call-done = bf16[1536,2048]{1,0:T(8,128)(2,1)} async-done(((bf16[192,2048]{1,0:T(8,128)(2,1)}), bf16[1536,2048]{1,0:T(8,128)(2,1)}) %all-gather.14.cloned.1.call-update) | async-done | bytes 6291472 | tf_op jit(solution)/shard_map/all_gather | solution.py:79
  127.3 16.3 gather_fusion.1
  143.5 9.7 fusion.39
  187.2 16.3 gather_fusion.3
  210.5 61.5 %reduce-scatter.13.cloned.1.call-done = bf16[192,2048]{1,0:T(8,128)(2,1)} async-done(((bf16[1536,2048]{1,0:T(8,128)(2,1)}), bf16[192,2048]{1,0:T(8,128)(2,1)}) %reduce-scatter.13.cloned.1.call-update) | async-done | bytes 786448 | tf_op jit(solution)/shard_map/reduce_scatter | solution.py:87
  280.4 44.8 %all-gather.22.cloned.1.call-done = bf16[1024,2048]{1,0:T(8,128)(2,1)} async-done(((bf16[1024,512]{1,0:T(8,128)(2,1)}), bf16[1024,2048]{1,0:T(8,128)(2,1)}) %all-gather.22.cloned.1.call-update) | async-done | bytes 4194320 | tf_op jit(solution)/shard_map/all_gather | solution.py:173
  342.0 73.0 %all-gather.18.cloned.1.call-done = bf16[2,2048,1024]{2,1,0:T(8,128)(2,1)} async-done(((bf16[2,512,1024]{2,1,0:T(8,128)(2,1)}), bf16[2,2048,1024]{2,1,0:T(8,128)(2,1)}) %all-gather.18.cloned.1.call-update) | async-done | bytes 8388624 | tf_op jit(solution)/shard_map/all_gather | solution.py:172
  431.0 7.9 pad_maximum_fusion.1
  454.3 27.4 %all-gather.20.cloned.1.call-done = bf16[1536,2048]{1,0:T(8,128)(2,1)} async-done(((bf16[192,2048]{1,0:T(8,128)(2,1)}), bf16[1536,2048]{1,0:T(8,128)(2,1)}) %all-gather.20.cloned.1.call-update) | async-done | bytes 6291472 | tf_op jit(solution)/shard_map/all_gather | solution.py:79
  481.8 19.2 %convolution_bitcast_fusion.3 = f32[2,1536,1024]{1,2,0:T(8,128)} fusion(bf16[2,2048,1024]{2,1,0:T(8,128)(2,1)} %bitcast_select_fusion.1, bf16[1536,2048]{1,0:T(8,128)(2,1)} %all-gather.20.cloned.1.call-done), kind=kOutput, calls=%fused_computation.38 | convolution fusion | flops 12884901888 | bytes 27262976 | tf_op jit(solution)/shard_map/td,sdf->stf/dot_general | solution.py:234
  501.0 14.3 convolution_convert_fusion.1
  519.4 27.3 %all-gather.32.cloned.1.call-done = bf16[1,1536,2048]{2,1,0:T(8,128)(2,1)} async-done(((bf16[1,192,2048]{2,1,0:T(8,128)(2,1)}), bf16[1,1536,2048]{2,1,0:T(8,128)(2,1)}) %all-gather.32.cloned.1.call-update) | async-done | bytes 6291472 | tf_op jit(solution)/shard_map/all_gather | solution.py:83
  546.8 14.9 fusion.71
  564.3 17.7 %bitcast_convert_fusion.1 = bf16[1536,2048]{1,0:T(8,128)(2,1)} fusion(bf16[2,2048,1024]{2,1,0:T(8,128)(2,1)} %bitcast_select_fusion.1, bf16[1,1536,1024]{1,2,0:T(8,128)(2,1)S(1)} %get-tuple-element.268, bf16[1,1536,1024]{1,2,0:T(8,128)(2,1)S(1)} %get-tuple-element.267), kind=kOutput, calls=%fused_computation.29 | convolution fusion | flops 12891193344 | bytes 20971520 | tf_op jit(solution)/shard_map/stf,sdf->td/dot_general | solution.py:251
  582.7 34.8 %reduce-scatter.15.cloned.1.call-done = bf16[192,2048]{1,0:T(8,128)(2,1)} async-done(((bf16[1536,2048]{1,0:T(8,128)(2,1)}), bf16[192,2048]{1,0:T(8,128)(2,1)}) %reduce-scatter.15.cloned.1.call-update) | async-done | bytes 786448 | tf_op jit(solution)/shard_map/reduce_scatter | solution.py:87
  617.5 70.5 %reduce-scatter.21.cloned.1.call-done = bf16[192,2048]{1,0:T(8,128)(2,1)} async-done(((bf16[1536,2048]{1,0:T(8,128)(2,1)}), bf16[192,2048]{1,0:T(8,128)(2,1)}) %reduce-scatter.21.cloned.1.call-update) | async-done | bytes 786448 | tf_op jit(solution)/shard_map/reduce_scatter | solution.py:93
  694.7 62.5 %all-gather.24.cloned.1.call-done = bf16[1536,2048]{1,0:T(8,128)(2,1)} async-done(((bf16[192,2048]{1,0:T(8,128)(2,1)}), bf16[1536,2048]{1,0:T(8,128)(2,1)}) %all-gather.24.cloned.1.call-update) | async-done | bytes 6291472 | tf_op jit(solution)/shard_map/all_gather | solution.py:79
  757.2 16.3 gather_fusion.5
  773.5 9.7 fusion.32
  811.6 16.3 gather_fusion.6
  830.5 17.1 %gather_fusion.7 = bf16[1536,2048]{1,0:T(8,128)(2,1)} fusion(bf16[1536,2048]{1,0:T(8,128)(2,1)} %all-gather.28.cloned.1.call-done, s32[2048]{0:T(1024)S(1)} %copy-done.87), kind=kCustom, calls=%fused_computation.7 | custom fusion | bytes 12589056 | tf_op jit(solution)/shard_map/gather | solution.py:254
  880.5 9.7 convolution_bitcast_fusion.1
  890.2 16.4 gather_fusion.8
  906.7 68.0 %reduce-scatter.23.cloned.1.call-done = bf16[192,2048]{1,0:T(8,128)(2,1)} async-done(((bf16[1536,2048]{1,0:T(8,128)(2,1)}), bf16[192,2048]{1,0:T(8,128)(2,1)}) %reduce-scatter.23.cloned.1.call-update) | async-done | bytes 786448 | tf_op jit(solution)/shard_map/reduce_scatter | solution.py:93
  979.6 62.7 %all-gather.26.cloned.1.call-done = bf16[1536,2048]{1,0:T(8,128)(2,1)} async-done(((bf16[192,2048]{1,0:T(8,128)(2,1)}), bf16[1536,2048]{1,0:T(8,128)(2,1)}) %all-gather.26.cloned.1.call-update) | async-done | bytes 6291472 | tf_op jit(solution)/shard_map/all_gather | solution.py:79
  1042.3 19.2 %convolution_bitcast_fusion.2 = f32[2,1536,1024]{1,2,0:T(8,128)} fusion(bf16[2,2048,1024]{2,1,0:T(8,128)(2,1)} %bitcast_select_fusion.1, bf16[1536,2048]{1,0:T(8,128)(2,1)} %all-gather.26.cloned.1.call-done), kind=kOutput, calls=%fused_computation.37 | convolution fusion | flops 12884901888 | bytes 27262976 | tf_op jit(solution)/shard_map/td,sdf->stf/dot_general | solution.py:234
  1061.5 46.2 %all-gather.34.cloned.1.call-done = bf16[1,1536,2048]{2,1,0:T(8,128)(2,1)} async-done(((bf16[1,192,2048]{2,1,0:T(8,128)(2,1)}), bf16[1,1536,2048]{2,1,0:T(8,128)(2,1)}) %all-gather.34.cloned.1.call-update) | async-done | bytes 6291472 | tf_op jit(solution)/shard_map/all_gather | solution.py:83
  1107.7 15.1 fusion.72
  1125.4 17.8 %bitcast_convert_fusion = bf16[1536,2048]{1,0:T(8,128)(2,1)} fusion(bf16[2,2048,1024]{2,1,0:T(8,128)(2,1)} %bitcast_select_fusion.1, bf16[1,1536,1024]{1,2,0:T(8,128)(2,1)S(1)} %get-tuple-element.266, bf16[1,1536,1024]{1,2,0:T(8,128)(2,1)S(1)} %get-tuple-element.265), kind=kOutput, calls=%fused_computation.28 | convolution fusion | flops 12891193344 | bytes 20971520 | tf_op jit(solution)/shard_map/stf,sdf->td/dot_general | solution.py:251
  1143.3 15.1 convolution_convert_fusion
  1158.9 52.9 %reduce-scatter.25.cloned.1.call-done = bf16[192,2048]{1,0:T(8,128)(2,1)} async-done(((bf16[1536,2048]{1,0:T(8,128)(2,1)}), bf16[192,2048]{1,0:T(8,128)(2,1)}) %reduce-scatter.25.cloned.1.call-update) | async-done | bytes 786448 | tf_op jit(solution)/shard_map/reduce_scatter | solution.py:93
  1213.7 68.5 %reduce-scatter.19.cloned.1.call-done = bf16[192,2048]{1,0:T(8,128)(2,1)} async-done(((bf16[1536,2048]{1,0:T(8,128)(2,1)}), bf16[192,2048]{1,0:T(8,128)(2,1)}) %reduce-scatter.19.cloned.1.call-update) | async-done | bytes 786448 | tf_op jit(solution)/shard_map/reduce_scatter | solution.py:87
  1286.7 11.7 fusion.11
  1298.4 13.1 fusion.46
  1336.7 19.7 %fusion.34 = f32[2,1024,2048]{2,1,0:T(8,128)} fusion(bf16[1536,2048]{1,0:T(8,128)(2,1)} %all-gather.20.cloned.1.call-done, bf16[1,1536,1024]{1,2,0:T(8,128)(2,1)} %copy-done.152, bf16[1,1536,1024]{1,2,0:T(8,128)(2,1)S(1)} %copy-done.151), kind=kOutput, calls=%fused_computation.87 | convolution fusion | flops 12888047616 | bytes 29360128 | tf_op jit(solution)/shard_map/td,stf->sdf/dot_general | solution.py:247
  1356.4 22.3 %add_bitcast_fusion = bf16[2,2048,1024]{1,2,0:T(8,128)(2,1)} fusion(f32[2,1024,2048]{2,1,0:T(8,128)} %fusion.34, bf16[1536,2048]{1,0:T(8,128)(2,1)} %all-gather.26.cloned.1.call-done, bf16[1,1536,1024]{1,2,0:T(8,128)(2,1)} %copy-done.154, bf16[1,1536,1024]{1,2,0:T(8,128)(2,1)} %copy-done.153), kind=kOutput, calls=%fused_computation.27 | convolution fusion | flops 12896436224 | bytes 37748736 | tf_op jit(solution)/shard_map/td,stf->sdf/dot_general | solution.py:247
  1378.6 14.6 reshape.1437
  1393.3 8.2 fusion.251
  1442.2 8.2 fusion
  1457.5 16.4 gather_fusion.9
  1528.4 9.3 add_bitcast_fusion.1
  1549.5 9.0 convolution_bitcast_fusion
  1558.6 16.4 gather_fusion.10
  1586.5 10.7 multiply_subtract_fusion
  1602.6 11.3 reduce-scatter.29.cloned.1.call-done
  1619.5 66.4 %reduce-scatter.27.cloned.1.call-done = bf16[192,2048]{1,0:T(8,128)(2,1)} async-done(((bf16[1536,2048]{1,0:T(8,128)(2,1)}), bf16[192,2048]{1,0:T(8,128)(2,1)}) %reduce-scatter.27.cloned.1.call-update) | async-done | bytes 786448 | tf_op jit(solution)/shard_map/reduce_scatter | solution.py:93
  (634 shorter events, 428.4 us)
Async XLA Ops:
  7.2 53.1 %all-gather.16.cloned.1.call-start = ((), (), s32[]{:S(2)}) async-start(), calls=%async_computation.13 | async-start | bytes 1310720 | tf_op jit(solution)/shard_map/all_gather | solution.py:171
  9.5 117.8 %all-gather.14.cloned.1.call-start = ((), (), s32[]{:S(2)}) async-start(), calls=%async_computation.12 | async-start | bytes 7077888 | tf_op jit(solution)/shard_map/all_gather | solution.py:79
  12.8 259.2 %reduce-scatter.13.cloned.1.call-start = ((), (), s32[]{:S(2)}) async-start(), calls=%async_computation.14 | async-start | bytes 7077888 | tf_op jit(solution)/shard_map/reduce_scatter | solution.py:87
  15.3 33.5 %copy-start.36 = (bf16[3,512,256]{2,1,0:T(8,128)(2,1)}, bf16[3,512,256]{2,1,0:T(8,128)(2,1)S(1)}, u32[]{:S(2)}) copy-start(bf16[3,512,256]{2,1,0:T(8,128)(2,1)S(1)} %get-tuple-element.264) | copy-start | bytes 2359300
  15.3 23.5 %collective-permute-start = (bf16[3,512,256]{2,1,0:T(8,128)(2,1)S(1)}, bf16[3,512,256]{2,1,0:T(8,128)(2,1)S(1)}, u32[]{:S(2)}, u32[]{:S(2)}) collective-permute-start(bf16[3,512,256]{2,1,0:T(8,128)(2,1)S(1)} %get-tuple-element.264), channel_id=1, source_target_pairs={{0,24},{8,0},{16,8},{24,16},{1,25},{9,1},{17,9},{25,17},{2,26},{10... | collective-permute-start | bytes 2359304 | tf_op jit(solution)/shard_map/ppermute | solution.py:164
  19.8 259.4 %copy-start.146 = (s32[4]{0:T(128)}, s32[4]{0:T(128)S(1)}, u32[]{:S(2)}) copy-start(s32[4]{0:T(128)S(1)} %get-tuple-element.330) | copy-start | bytes 52
  34.7 92.5 %copy-start.86 = (s32[2048]{0:T(1024)}, s32[2048]{0:T(1024)S(1)}, u32[]{:S(2)}) copy-start(s32[2048]{0:T(1024)S(1)} %pad_clamp_fusion.3) | copy-start | bytes 24580
  35.4 151.7 %copy-start.92 = (s32[2048]{0:T(1024)}, s32[2048]{0:T(1024)S(1)}, u32[]{:S(2)}) copy-start(s32[2048]{0:T(1024)S(1)} %get-tuple-element.370) | copy-start | bytes 24580
  35.7 28.8 %copy-start.132 = (pred[4]{0:T(512)(128)(4,1)}, pred[4]{0:T(512)(128)(4,1)S(1)}, u32[]{:S(2)}) copy-start(pred[4]{0:T(512)(128)(4,1)S(1)} %get-tuple-element.364) | copy-start | bytes 16
  40.1 41.7 %collective-permute-start.1 = (bf16[3,1024,256]{2,1,0:T(8,128)(2,1)}, bf16[3,1024,256]{2,1,0:T(8,128)(2,1)}, u32[]{:S(2)}, u32[]{:S(2)}) collective-permute-start(bf16[3,1024,256]{2,1,0:T(8,128)(2,1)} %pad_maximum_fusion.9), channel_id=1, source_target_pairs={{0,16},{8,24},{16,0},{24,8},{1,17},{9,25},{17,1},{25,9},{2,18},{10... | collective-permute-start | bytes 4718600 | tf_op jit(solution)/shard_map/ppermute | solution.py:164
  68.0 114.3 %copy-start.31 = (bf16[256,4,512]{0,2,1:T(8,128)(2,1)}, bf16[256,4,512]{0,2,1:T(8,128)(2,1)S(1)}, u32[]{:S(2)}) copy-start(bf16[256,4,512]{0,2,1:T(8,128)(2,1)S(1)} %copy.216) | copy-start | bytes 3145732
  203.5 121.7 %all-gather.22.cloned.1.call-start = ((), (), s32[]{:S(2)}) async-start(), calls=%async_computation.17 | async-start | bytes 5242880 | tf_op jit(solution)/shard_map/all_gather | solution.py:173
  206.2 208.7 %all-gather.18.cloned.1.call-start = ((), (), s32[]{:S(2)}) async-start(), calls=%async_computation.15 | async-start | bytes 10485760 | tf_op jit(solution)/shard_map/all_gather | solution.py:172
  210.5 271.3 %all-gather.20.cloned.1.call-start = ((), (), s32[]{:S(2)}) async-start(), calls=%async_computation.16 | async-start | bytes 7077888 | tf_op jit(solution)/shard_map/all_gather | solution.py:79
  276.3 270.5 %all-gather.32.cloned.1.call-start = ((), (), s32[]{:S(2)}) async-start(), calls=%async_computation.33 | async-start | bytes 7077888 | tf_op jit(solution)/shard_map/all_gather | solution.py:83
  279.1 338.4 %reduce-scatter.15.cloned.1.call-start = ((), (), s32[]{:S(2)}) async-start(), calls=%async_computation.18 | async-start | bytes 7077888 | tf_op jit(solution)/shard_map/reduce_scatter | solution.py:87
  515.3 172.7 %reduce-scatter.21.cloned.1.call-start = ((), (), s32[]{:S(2)}) async-start(), calls=%async_computation.23 | async-start | bytes 7077888 | tf_op jit(solution)/shard_map/reduce_scatter | solution.py:93
  582.1 175.2 %all-gather.24.cloned.1.call-start = ((), (), s32[]{:S(2)}) async-start(), calls=%async_computation.19 | async-start | bytes 7077888 | tf_op jit(solution)/shard_map/all_gather | solution.py:79
  582.7 111.2 %copy-start.111 = (f32[192]{0:T(256)}, f32[192]{0:T(256)S(1)}, u32[]{:S(2)}) copy-start(f32[192]{0:T(256)S(1)} %broadcast_multiply_fusion.9) | copy-start | bytes 2308
  693.9 136.6 %all-gather.28.cloned.1.call-start = ((), (), s32[]{:S(2)}) async-start(), calls=%async_computation.24 | async-start | bytes 7077888 | tf_op jit(solution)/shard_map/all_gather | solution.py:83
  694.7 212.0 %reduce-scatter.17.cloned.1.call-start = ((), (), s32[]{:S(2)}) async-start(), calls=%async_computation.20 | async-start | bytes 7077888 | tf_op jit(solution)/shard_map/reduce_scatter | solution.py:87
  694.7 78.8 %copy-start.88 = (s32[2048]{0:T(1024)}, s32[2048]{0:T(1024)S(1)}, u32[]{:S(2)}) copy-start(s32[2048]{0:T(1024)S(1)} %pad_clamp_fusion.1) | copy-start | bytes 24580
  694.7 78.8 %copy-start.57 = (bf16[3,2048,256]{2,1,0:T(8,128)(2,1)S(1)}, bf16[3,2048,256]{2,1,0:T(8,128)(2,1)}, u32[]{:S(2)}) copy-start(bf16[3,2048,256]{2,1,0:T(8,128)(2,1)} %bitcast_select_fusion.5) | copy-start | bytes 9437188
  828.0 146.6 %reduce-scatter.23.cloned.1.call-start = ((), (), s32[]{:S(2)}) async-start(), calls=%async_computation.25 | async-start | bytes 7077888 | tf_op jit(solution)/shard_map/reduce_scatter | solution.py:93
  906.6 68.1 %copy-start.1 = (bf16[2,192,2048]{2,1,0:T(8,128)(2,1)S(1)}, bf16[2,192,2048]{2,1,0:T(8,128)(2,1)}, u32[]{:S(2)}) copy-start(bf16[2,192,2048]{2,1,0:T(8,128)(2,1)} %param.49) | copy-start | bytes 4718596
  906.6 68.1 %copy-start.109 = (f32[192]{0:T(256)S(1)}, f32[192]{0:T(256)}, u32[]{:S(2)}) copy-start(f32[192]{0:T(256)} %copy-done.108) | copy-start | bytes 2308
  906.6 68.1 %copy-start.126 = (f32[192]{0:T(256)S(1)}, f32[192]{0:T(256)}, u32[]{:S(2)}) copy-start(f32[192]{0:T(256)} %copy-done.125) | copy-start | bytes 2308
  906.6 135.7 %all-gather.26.cloned.1.call-start = ((), (), s32[]{:S(2)}) async-start(), calls=%async_computation.21 | async-start | bytes 7077888 | tf_op jit(solution)/shard_map/all_gather | solution.py:79
  906.7 70.7 %copy-start.30 = (bf16[192,2048]{1,0:T(8,128)(2,1)S(1)}, bf16[192,2048]{1,0:T(8,128)(2,1)}, u32[]{:S(2)}) copy-start(bf16[192,2048]{1,0:T(8,128)(2,1)} %reduce-scatter.17.cloned.1.call-done) | copy-start | bytes 2359300
  979.0 128.8 %all-gather.34.cloned.1.call-start = ((), (), s32[]{:S(2)}) async-start(), calls=%async_computation.34 | async-start | bytes 7077888 | tf_op jit(solution)/shard_map/all_gather | solution.py:83
  979.5 232.2 %reduce-scatter.25.cloned.1.call-start = ((), (), s32[]{:S(2)}) async-start(), calls=%async_computation.26 | async-start | bytes 7077888 | tf_op jit(solution)/shard_map/reduce_scatter | solution.py:93
  1143.3 138.9 %reduce-scatter.19.cloned.1.call-start = ((), (), s32[]{:S(2)}) async-start(), calls=%async_computation.22 | async-start | bytes 7077888 | tf_op jit(solution)/shard_map/reduce_scatter | solution.py:87
  1158.5 299.0 %all-gather.30.cloned.1.call-start = ((), (), s32[]{:S(2)}) async-start(), calls=%async_computation.27 | async-start | bytes 7077888 | tf_op jit(solution)/shard_map/all_gather | solution.py:83
  1213.6 72.9 %copy-start.141 = (pred[4]{0:T(512)(128)(4,1)S(1)}, pred[4]{0:T(512)(128)(4,1)}, u32[]{:S(2)}) copy-start(pred[4]{0:T(512)(128)(4,1)} %get-tuple-element.320) | copy-start | bytes 16
  1213.6 73.0 %copy-start.140 = (pred[4]{0:T(512)(128)(4,1)S(1)}, pred[4]{0:T(512)(128)(4,1)}, u32[]{:S(2)}) copy-start(pred[4]{0:T(512)(128)(4,1)} %get-tuple-element.323) | copy-start | bytes 16
  1213.6 73.0 %copy-start.147 = (s32[4]{0:T(128)S(1)}, s32[4]{0:T(128)}, u32[]{:S(2)}) copy-start(s32[4]{0:T(128)} %copy-done.146) | copy-start | bytes 52
  1213.6 73.0 %copy-start.149 = (s32[4]{0:T(128)S(1)}, s32[4]{0:T(128)}, u32[]{:S(2)}) copy-start(s32[4]{0:T(128)} %copy-done.148) | copy-start | bytes 52
  1286.4 292.0 %reduce-scatter.35.cloned.1.call-start = ((), (), s32[]{:S(2)}) async-start(), calls=%async_computation.32 | async-start | bytes 5242880 | tf_op jit(solution)/shard_map/reduce_scatter | solution.py:118
  1334.8 251.6 %reduce-scatter.33.cloned.1.call-start = ((), (), s32[]{:S(2)}) async-start(), calls=%async_computation.31 | async-start | bytes 10485760 | tf_op jit(solution)/shard_map/reduce_scatter | solution.py:112
  1450.5 146.7 %reduce-scatter.31.cloned.1.call-start = ((), (), s32[]{:S(2)}) async-start(), calls=%async_computation.30 | async-start | bytes 1310720 | tf_op jit(solution)/shard_map/reduce_scatter | solution.py:106
  1520.1 93.7 %reduce-scatter.29.cloned.1.call-start = ((), (), s32[]{:S(2)}) async-start(), calls=%async_computation.29 | async-start | bytes 3932160 | tf_op jit(solution)/shard_map/reduce_scatter | solution.py:100
  1547.7 138.2 %reduce-scatter.27.cloned.1.call-start = ((), (), s32[]{:S(2)}) async-start(), calls=%async_computation.28 | async-start | bytes 7077888 | tf_op jit(solution)/shard_map/reduce_scatter | solution.py:93
  1602.5 83.4 %copy-start.2 = (bf16[2,192,2048]{2,1,0:T(8,128)(2,1)S(1)}, bf16[2,192,2048]{2,1,0:T(8,128)(2,1)}, u32[]{:S(2)}) copy-start(bf16[2,192,2048]{2,1,0:T(8,128)(2,1)} %param.49) | copy-start | bytes 4718596
  1602.6 83.4 %copy-start.112 = (f32[192]{0:T(256)S(1)}, f32[192]{0:T(256)}, u32[]{:S(2)}) copy-start(f32[192]{0:T(256)} %copy-done.111) | copy-start | bytes 2308
  1602.6 83.4 %copy-start.129 = (f32[192]{0:T(256)S(1)}, f32[192]{0:T(256)}, u32[]{:S(2)}) copy-start(f32[192]{0:T(256)} %copy-done.128) | copy-start | bytes 2308
  1602.6 85.1 %copy-start.47 = (f32[192,2048]{1,0:T(8,128)S(1)}, f32[192,2048]{1,0:T(8,128)}, u32[]{:S(2)}) copy-start(f32[192,2048]{1,0:T(8,128)} %get-tuple-element.262) | copy-start | bytes 4718596
  1602.6 85.1 %copy-start.110 = (f32[192]{0:T(256)S(1)}, f32[192]{0:T(256)}, u32[]{:S(2)}) copy-start(f32[192]{0:T(256)} %copy-done.108) | copy-start | bytes 2308
  1602.6 85.1 %copy-start.127 = (f32[192]{0:T(256)S(1)}, f32[192]{0:T(256)}, u32[]{:S(2)}) copy-start(f32[192]{0:T(256)} %copy-done.125) | copy-start | bytes 2308
  (138 other events, 513.9 us)
Sparse Core Ops, SparseCore 0:
  10.4 49.8 all-gather.15
  62.5 64.6 all-gather.13
  203.6 68.3 reduce-scatter.12
  274.3 50.8 all-gather.21
  327.4 87.4 all-gather.17
  417.0 64.6 all-gather.19
  483.4 63.3 all-gather.31
  549.1 68.3 reduce-scatter.14
  619.8 68.1 reduce-scatter.20
  694.0 63.1 all-gather.23
  759.4 63.3 all-gather.27
  828.1 68.4 reduce-scatter.16
  906.7 67.8 reduce-scatter.22
  979.1 63.1 all-gather.25
  1044.3 63.3 all-gather.33
  1143.4 68.3 reduce-scatter.24
  1213.9 68.1 reduce-scatter.18
  1286.6 63.1 all-gather.29
  1352.7 51.2 reduce-scatter.34
  1450.6 84.8 reduce-scatter.32
  1539.0 27.9 reduce-scatter.30
  1569.9 43.8 reduce-scatter.28
  1616.2 69.7 reduce-scatter.26
